TPU v7x, 32 devices: a whole 2x2x4 slice. The times are simulated.
32 devices in a mesh: cuts: 2 (over y), vec: 4 (over z), space: 2 (over x), rep: 2 (over core).
Axes of the slice: x: 2, y: 2, z: 4, core: 2. Of those that a mesh axis runs over, the one named last changes fastest.
Arguments:
- colour_vectors: float32 [256, 2, 3, 6, 2304], P(('cuts', 'vec'), None, None, 'space', 'rep'), parts along dimension 0, may hold values from -6 to 6
- gauge_links: float32 [3, 2, 3, 3, 12, 2304], P(None, None, None, None, ('cuts', 'space'), 'rep'), parts along dimension 4, may hold values from -1 to 1, as said below
Outputs:
- filtered: float32 [256, 2, 3, 6, 2304], P(('cuts', 'vec'), None, None, 'space', 'rep'), parts along dimension 0
- gram_matrix: float32 [2, 256, 128], P(None, ('cuts', 'vec')), parts along dimension 1
- projected: float32 [2, 256, 128], P(None, ('cuts', 'vec')), parts along dimension 1
There are 2 independent parts, one for each index of `cuts`. A program takes and returns all parts, laid end to end along the dimension named above; each array names one. Nothing has to cross between parts.
Inputs may be any that keep to these rules, and one draw needn't show every extreme that they name: `gauge_links`: each link is a unitary 3 x 3 complex matrix.
All inputs are finite; a program needn't handle non-finite values.
Results may differ from a plain program's by a relative error of at most 0.00017.
Values sent between devices are 32-bit elements; how exact they have to be, the bound alone decides.
A program may use at most 128 MiB of HBM per device.

v0:
```python
import jax
import jax.numpy as jnp
from jax import lax
from jax.sharding import PartitionSpec as P

LX = 48
LY = 48
DEG = 8


def from_behind(block, axis, distance):
    devices = range(lax.axis_size(axis))
    route = [((i - distance) % len(devices), i) for i in devices]
    return lax.ppermute(block, axis, route)


def with_halo(cells, sides, width):
    for axis, dim in sides:
        count = lax.axis_size(axis)
        head = lax.slice_in_dim(cells, 0, width, axis=dim)
        tail = lax.slice_in_dim(cells, cells.shape[dim] - width, cells.shape[dim], axis=dim)
        cells = jnp.concatenate(
            [
                lax.ppermute(tail, axis, [(i, (i + 1) % count) for i in range(count)]),
                cells,
                lax.ppermute(head, axis, [((i + 1) % count, i) for i in range(count)]),
            ],
            axis=dim,
        )
    return cells


def apply_link(link, source, dagger):
    link_real = link[0]
    link_imag = link[1]
    vec_real = source[:, 0]
    vec_imag = source[:, 1]
    out_real = jnp.zeros_like(vec_real)
    out_imag = jnp.zeros_like(vec_imag)
    for column in range(3):
        if dagger:
            mat_real = link_real[column]
            mat_imag = -link_imag[column]
        else:
            mat_real = link_real[:, column]
            mat_imag = link_imag[:, column]
        src_real = vec_real[:, column][:, None]
        src_imag = vec_imag[:, column][:, None]
        out_real = out_real + (mat_real[None] * src_real - mat_imag[None] * src_imag)
        out_imag = out_imag + (mat_real[None] * src_imag + mat_imag[None] * src_real)
    return jnp.stack([out_real, out_imag], axis=1)


def inner_product(left_matrix, right_matrix):
    return lax.dot_general(
        left_matrix,
        right_matrix,
        (((1,), (1,)), ((), ())),
        precision=lax.Precision.HIGHEST,
        preferred_element_type=jnp.float32,
    )


def block_pair(left_field, right_field):
    left_real = left_field[:, 0].reshape(left_field.shape[0], -1)
    left_imag = left_field[:, 1].reshape(left_field.shape[0], -1)
    right_real = right_field[:, 0].reshape(right_field.shape[0], -1)
    right_imag = right_field[:, 1].reshape(right_field.shape[0], -1)
    real_part = inner_product(left_real, right_real) + inner_product(left_imag, right_imag)
    imag_part = inner_product(left_real, right_imag) - inner_product(left_imag, right_real)
    return jnp.stack([real_part, imag_part])


def chebyshev(start_vectors, hop_fn):

    def filter_map(source):
        return -(source + 2.0 * hop_fn(source)) / 11.0

    previous = start_vectors
    current = filter_map(previous)
    for degree in range(DEG - 1):
        following = 2.0 * filter_map(current) - previous
        previous = current
        current = following
    return (current, 6.0 * current - hop_fn(current))


def body(colour_vectors, gauge_links):
    flat_width = colour_vectors.shape[-1]
    local_count = colour_vectors.shape[0]
    rim_z = from_behind(gauge_links[2][:, :, :, -1:, :], "space", 1)
    lower_z = jnp.concatenate([rim_z, gauge_links[2][:, :, :, :-1, :]], axis=3)
    rim_x = from_behind(gauge_links[0][:, :, :, :, flat_width - LY :], "rep", 1)
    lower_x = jnp.concatenate([rim_x, gauge_links[0][:, :, :, :, : flat_width - LY]], axis=4)
    positions = lax.broadcasted_iota(jnp.int32, (flat_width,), 0) % LY
    last_y = positions == LY - 1
    first_y = positions == 0

    def hopping(source):
        padded_x = with_halo(source, (("rep", 4),), LY)
        padded_z = with_halo(source, (("space", 3),), 1)
        summed = apply_link(gauge_links[0], padded_x[..., 2 * LY :], False) + apply_link(
            lower_x, padded_x[..., :flat_width], True
        )
        ahead_y = jnp.where(last_y, jnp.roll(source, LY - 1, -1), jnp.roll(source, -1, -1))
        summed = summed + apply_link(gauge_links[1], ahead_y, False)
        backward_y = apply_link(gauge_links[1], source, True)
        summed = summed + jnp.where(
            first_y, jnp.roll(backward_y, 1 - LY, -1), jnp.roll(backward_y, 1, -1)
        )
        summed = (
            summed
            + apply_link(gauge_links[2], padded_z[:, :, :, 2:], False)
            + apply_link(lower_z, padded_z[:, :, :, :-2], True)
        )
        return summed

    filtered, laplace_image = chebyshev(colour_vectors, hopping)
    site_count = float(LX * LY * colour_vectors.shape[3] * lax.axis_size("space"))
    vec_count = lax.axis_size("vec")
    vec_index = lax.axis_index("vec")
    total_vectors = local_count * vec_count

    def add_blocks(turn_index, moving_panel, gram_rows, image_rows):
        owner_index = (vec_index - turn_index + vec_count) % vec_count
        gram_rows = lax.dynamic_update_slice(
            gram_rows, block_pair(filtered, moving_panel), (0, 0, owner_index * local_count)
        )
        image_rows = lax.dynamic_update_slice(
            image_rows, block_pair(laplace_image, moving_panel), (0, 0, owner_index * local_count)
        )
        return (gram_rows, image_rows)

    def visit(turn_index, state_tuple):
        moving_panel, gram_rows, image_rows = state_tuple
        gram_rows, image_rows = add_blocks(turn_index, moving_panel, gram_rows, image_rows)
        moving_panel = from_behind(moving_panel, "vec", 1)
        return (moving_panel, gram_rows, image_rows)

    empty_rows = jnp.zeros((2, local_count, total_vectors), jnp.float32)
    moving_panel, gram_rows, image_rows = lax.fori_loop(
        0, vec_count - 1, visit, (filtered, empty_rows, empty_rows)
    )
    gram_rows, image_rows = add_blocks(vec_count - 1, moving_panel, gram_rows, image_rows)
    gram_rows, image_rows = lax.psum((gram_rows, image_rows), ("space", "rep"))
    return (filtered, gram_rows / site_count, image_rows / site_count)


def solution(mesh):
    return jax.shard_map(
        body,
        mesh=mesh,
        in_specs=(
            P(("cuts", "vec"), None, None, "space", "rep"),
            P(None, None, None, None, ("cuts", "space"), "rep"),
        ),
        out_specs=(
            P(("cuts", "vec"), None, None, "space", "rep"),
            P(None, ("cuts", "vec"), None),
            P(None, ("cuts", "vec"), None),
        ),
        check_vma=False,
    )
```

profile of v0, /device:TPU:0, one launch (start us, length us, event | category | flops | bytes accessed | tf_op | source)
XLA Modules:
  0.0 728.6 jit_solution(12017337156248696018)
XLA Ops:
  7.2 2.0 copy.56
  13.3 2.6 collective-permute-start.6
  20.3 2.5 subtract_add_fusion.51
  24.1 2.0 collective-permute-start.5
  26.1 1.8 fusion.352
  28.1 29.0 %collective-permute-done.5 = f32[2,3,3,1,1152]{4,0,3,2,1:T(2,128)S(1)} collective-permute-done((f32[2,3,3,1,1152]{4,0,3,2,1:T(2,128)}, f32[2,3,3,1,1152]{4,0,3,2,1:T(2,128)S(1)}, u32[]{:S(2)}, u32[]{:S(2)}) %collective-permute-start.5) | collective-permute-done | bytes 82976 | tf_op jit(solution)/shard_map/ppermute | solution.py:14
  58.4 1.9 maximum_bitcast_fusion.32
  73.4 1.9 fusion.213
  76.5 1.8 collective-permute-start.10
  82.3 16.8 %collective-permute-done.10 = f32[32,2,3,1,1152]{4,0,3,2,1:T(8,128)S(1)} collective-permute-done((f32[32,2,3,1,1152]{4,0,3,2,1:T(8,128)S(1)}, f32[32,2,3,1,1152]{4,0,3,2,1:T(8,128)S(1)}, u32[]{:S(2)}, u32[]{:S(2)}) %collective-permute-start.10) | collective-permute-done | bytes 884768 | tf_op jit(solution)/shard_map/ppermute | solution.py:24
  99.1 17.8 %collective-permute-done.9 = f32[32,2,3,1,1152]{4,0,3,2,1:T(8,128)S(1)} collective-permute-done((f32[32,2,3,1,1152]{4,0,3,2,1:T(8,128)S(1)}, f32[32,2,3,1,1152]{4,0,3,2,1:T(8,128)S(1)}, u32[]{:S(2)}, u32[]{:S(2)}) %collective-permute-start.9) | collective-permute-done | bytes 884768 | tf_op jit(solution)/shard_map/ppermute | solution.py:26
  116.9 2.8 maximum_bitcast_fusion.28
  127.4 3.3 fusion.204
  136.8 17.7 %collective-permute-done.13 = f32[32,2,3,1,1152]{4,0,3,2,1:T(8,128)S(1)} collective-permute-done((f32[32,2,3,1,1152]{4,0,3,2,1:T(8,128)S(1)}, f32[32,2,3,1,1152]{4,0,3,2,1:T(8,128)S(1)}, u32[]{:S(2)}, u32[]{:S(2)}) %collective-permute-start.13) | collective-permute-done | bytes 884768 | tf_op jit(solution)/shard_map/ppermute | solution.py:26
  154.5 16.9 %collective-permute-done.14 = f32[32,2,3,1,1152]{4,0,3,2,1:T(8,128)S(1)} collective-permute-done((f32[32,2,3,1,1152]{4,0,3,2,1:T(8,128)S(1)}, f32[32,2,3,1,1152]{4,0,3,2,1:T(8,128)S(1)}, u32[]{:S(2)}, u32[]{:S(2)}) %collective-permute-start.14) | collective-permute-done | bytes 884768 | tf_op jit(solution)/shard_map/ppermute | solution.py:24
  171.4 2.5 maximum_bitcast_fusion.24
  181.8 3.7 fusion.194
  191.6 17.7 %collective-permute-done.17 = f32[32,2,3,1,1152]{4,0,3,2,1:T(8,128)S(1)} collective-permute-done((f32[32,2,3,1,1152]{4,0,3,2,1:T(8,128)S(1)}, f32[32,2,3,1,1152]{4,0,3,2,1:T(8,128)S(1)}, u32[]{:S(2)}, u32[]{:S(2)}) %collective-permute-start.17) | collective-permute-done | bytes 884768 | tf_op jit(solution)/shard_map/ppermute | solution.py:26
  209.3 16.0 %collective-permute-done.18 = f32[32,2,3,1,1152]{4,0,3,2,1:T(8,128)S(1)} collective-permute-done((f32[32,2,3,1,1152]{4,0,3,2,1:T(8,128)S(1)}, f32[32,2,3,1,1152]{4,0,3,2,1:T(8,128)S(1)}, u32[]{:S(2)}, u32[]{:S(2)}) %collective-permute-start.18) | collective-permute-done | bytes 884768 | tf_op jit(solution)/shard_map/ppermute | solution.py:24
  225.3 3.4 maximum_bitcast_fusion.20
  236.5 3.5 fusion.184
  246.1 17.7 %collective-permute-done.21 = f32[32,2,3,1,1152]{4,0,3,2,1:T(8,128)S(1)} collective-permute-done((f32[32,2,3,1,1152]{4,0,3,2,1:T(8,128)S(1)}, f32[32,2,3,1,1152]{4,0,3,2,1:T(8,128)S(1)}, u32[]{:S(2)}, u32[]{:S(2)}) %collective-permute-start.21) | collective-permute-done | bytes 884768 | tf_op jit(solution)/shard_map/ppermute | solution.py:26
  263.8 15.2 %collective-permute-done.22 = f32[32,2,3,1,1152]{4,0,3,2,1:T(8,128)S(1)} collective-permute-done((f32[32,2,3,1,1152]{4,0,3,2,1:T(8,128)S(1)}, f32[32,2,3,1,1152]{4,0,3,2,1:T(8,128)S(1)}, u32[]{:S(2)}, u32[]{:S(2)}) %collective-permute-start.22) | collective-permute-done | bytes 884768 | tf_op jit(solution)/shard_map/ppermute | solution.py:24
  279.0 2.4 maximum_bitcast_fusion.16
  289.1 3.3 fusion.174
  298.5 17.7 %collective-permute-done.25 = f32[32,2,3,1,1152]{4,0,3,2,1:T(8,128)S(1)} collective-permute-done((f32[32,2,3,1,1152]{4,0,3,2,1:T(8,128)S(1)}, f32[32,2,3,1,1152]{4,0,3,2,1:T(8,128)S(1)}, u32[]{:S(2)}, u32[]{:S(2)}) %collective-permute-start.25) | collective-permute-done | bytes 884768 | tf_op jit(solution)/shard_map/ppermute | solution.py:26
  316.2 14.3 %collective-permute-done.26 = f32[32,2,3,1,1152]{4,0,3,2,1:T(8,128)S(1)} collective-permute-done((f32[32,2,3,1,1152]{4,0,3,2,1:T(8,128)S(1)}, f32[32,2,3,1,1152]{4,0,3,2,1:T(8,128)S(1)}, u32[]{:S(2)}, u32[]{:S(2)}) %collective-permute-start.26) | collective-permute-done | bytes 884768 | tf_op jit(solution)/shard_map/ppermute | solution.py:24
  330.5 2.8 maximum_bitcast_fusion.12
  341.1 3.5 fusion.164
  350.7 17.7 %collective-permute-done.29 = f32[32,2,3,1,1152]{4,0,3,2,1:T(8,128)S(1)} collective-permute-done((f32[32,2,3,1,1152]{4,0,3,2,1:T(8,128)S(1)}, f32[32,2,3,1,1152]{4,0,3,2,1:T(8,128)S(1)}, u32[]{:S(2)}, u32[]{:S(2)}) %collective-permute-start.29) | collective-permute-done | bytes 884768 | tf_op jit(solution)/shard_map/ppermute | solution.py:26
  368.3 13.5 %collective-permute-done.30 = f32[32,2,3,1,1152]{4,0,3,2,1:T(8,128)S(1)} collective-permute-done((f32[32,2,3,1,1152]{4,0,3,2,1:T(8,128)S(1)}, f32[32,2,3,1,1152]{4,0,3,2,1:T(8,128)S(1)}, u32[]{:S(2)}, u32[]{:S(2)}) %collective-permute-start.30) | collective-permute-done | bytes 884768 | tf_op jit(solution)/shard_map/ppermute | solution.py:24
  381.8 3.4 maximum_bitcast_fusion.8
  393.0 3.7 fusion.154
  402.8 17.7 %collective-permute-done.33 = f32[32,2,3,1,1152]{4,0,3,2,1:T(8,128)S(1)} collective-permute-done((f32[32,2,3,1,1152]{4,0,3,2,1:T(8,128)S(1)}, f32[32,2,3,1,1152]{4,0,3,2,1:T(8,128)S(1)}, u32[]{:S(2)}, u32[]{:S(2)}) %collective-permute-start.33) | collective-permute-done | bytes 884768 | tf_op jit(solution)/shard_map/ppermute | solution.py:26
  420.5 12.6 %collective-permute-done.34 = f32[32,2,3,1,1152]{4,0,3,2,1:T(8,128)S(1)} collective-permute-done((f32[32,2,3,1,1152]{4,0,3,2,1:T(8,128)S(1)}, f32[32,2,3,1,1152]{4,0,3,2,1:T(8,128)S(1)}, u32[]{:S(2)}, u32[]{:S(2)}) %collective-permute-start.34) | collective-permute-done | bytes 884768 | tf_op jit(solution)/shard_map/ppermute | solution.py:24
  433.1 3.4 maximum_bitcast_fusion.4
  444.3 3.3 fusion.144
  455.2 16.2 %collective-permute-done.37 = f32[32,2,3,1,1152]{4,0,3,2,1:T(8,128)S(1)} collective-permute-done((f32[32,2,3,1,1152]{4,0,3,2,1:T(8,128)S(1)}, f32[32,2,3,1,1152]{4,0,3,2,1:T(8,128)S(1)}, u32[]{:S(2)}, u32[]{:S(2)}) %collective-permute-start.37) | collective-permute-done | bytes 884768 | tf_op jit(solution)/shard_map/ppermute | solution.py:26
  471.4 11.8 %collective-permute-done.38 = f32[32,2,3,1,1152]{4,0,3,2,1:T(8,128)S(1)} collective-permute-done((f32[32,2,3,1,1152]{4,0,3,2,1:T(8,128)S(1)}, f32[32,2,3,1,1152]{4,0,3,2,1:T(8,128)S(1)}, u32[]{:S(2)}, u32[]{:S(2)}) %collective-permute-start.38) | collective-permute-done | bytes 884768 | tf_op jit(solution)/shard_map/ppermute | solution.py:24
  483.2 2.5 maximum_bitcast_fusion
  492.7 3.5 fusion.134
  496.3 170.3 %while.19 = (s32[]{:T(128)}, f32[32,2,3,3,1152]{4,0,3,2,1:T(8,128)}, f32[2,32,128]{2,1,0:T(8,128)S(1)}, f32[2,32,128]{2,1,0:T(8,128)S(1)}, f32[32,2,3,3,1152]{4,...) while((s32[]{:T(128)}, ...), condition=%wide.region_1.2_spmd, body=%wide.region_0.1_spmd.sunk | while | flops 1019224064 | bytes 58556816 | solution.py:141
  496.5 1.8 copy.138
  498.2 2.8 fusion.431
  505.3 2.8 fusion.427
  512.3 41.9 %collective-permute-done = f32[32,2,3,3,1152]{4,0,3,2,1:T(8,128)} collective-permute-done((f32[32,2,3,3,1152]{4,0,3,2,1:T(8,128)S(1)}, f32[32,2,3,3,1152]{4,0,3,2,1:T(8,128)}, u32[]{:S(2)}, u32[]{:S(2)}) %collective-permute-start) | collective-permute-done | bytes 2654240 | tf_op jit(solution)/shard_map/while/body/eval_jaxpr/ppermute | solution.py:14
  554.2 1.8 copy.138
  556.0 2.8 fusion.431
  563.3 2.8 fusion.427
  570.6 41.3 %collective-permute-done = f32[32,2,3,3,1152]{4,0,3,2,1:T(8,128)} collective-permute-done((f32[32,2,3,3,1152]{4,0,3,2,1:T(8,128)S(1)}, f32[32,2,3,3,1152]{4,0,3,2,1:T(8,128)}, u32[]{:S(2)}, u32[]{:S(2)}) %collective-permute-start) | collective-permute-done | bytes 2654240 | tf_op jit(solution)/shard_map/while/body/eval_jaxpr/ppermute | solution.py:14
  612.0 1.8 copy.138
  613.7 2.8 fusion.431
  621.0 2.8 fusion.427
  628.4 37.9 %collective-permute-done = f32[32,2,3,3,1152]{4,0,3,2,1:T(8,128)} collective-permute-done((f32[32,2,3,3,1152]{4,0,3,2,1:T(8,128)S(1)}, f32[32,2,3,3,1152]{4,0,3,2,1:T(8,128)}, u32[]{:S(2)}, u32[]{:S(2)}) %collective-permute-start) | collective-permute-done | bytes 2654240 | tf_op jit(solution)/shard_map/while/body/eval_jaxpr/ppermute | solution.py:14
  666.5 3.2 fusion.278
  669.8 2.8 fusion.281
  672.6 2.6 fusion.272
  675.2 2.6 fusion.275
  677.8 2.6 fusion.305
  680.5 2.6 fusion.299
  683.1 2.6 fusion.317
  685.7 2.6 fusion.311
  690.2 3.5 copy.58
  693.7 24.8 %all-reduce.3.cloned.1.call-done = (f32[2,32,128]{2,1,0:T(8,128)}, f32[2,32,128]{2,1,0:T(8,128)}) async-done(((f32[2,32,128]{2,1,0:T(8,128)}, f32[2,32,128]{2,1,0:T(8,128)}), (f32[2,32,128]{2,1,0:T(8,128)}, f32[2,32,128]{2,1,0:T(8,128)})) %all-reduce.3.cloned.1.call-update) | async-done | bytes 65552 | tf_op jit(solution)/shard_map/psum | solution.py:145
  (453 shorter events, 164.0 us)
Async XLA Ops:
  7.2 711.4 %all-reduce.3.cloned.1.call-start = ((), (), s32[]{:S(2)}) async-start(), calls=%async_computation | async-start | bytes 131072 | tf_op jit(solution)/shard_map/psum | solution.py:145
  9.3 1.5 copy-start.23
  10.2 48.2 %collective-permute-start.3 = (f32[32,2,3,3,48]{4,0,3,2,1:T(8,128)}, f32[32,2,3,3,48]{4,0,3,2,1:T(8,128)}, u32[]{:S(2)}, u32[]{:S(2)}) collective-permute-start(f32[32,2,3,3,48]{4,0,3,2,1:T(8,128)} %get-tuple-element.508), channel_id=1, source_target_pairs={{0,1},{1,0},{2,3},{3,2},{4,5},{5,4},{6,7},{7,6},{8,9},{9,8},{10,11... | collective-permute-start | bytes 331784 | tf_op jit(solution)/shard_map/ppermute | solution.py:24
  11.6 14.5 %collective-permute-start.2 = (f32[2,3,3,3,48]{4,0,3,2,1:T(2,128)S(1)}, f32[2,3,3,3,48]{4,0,3,2,1:T(2,128)}, u32[]{:S(2)}, u32[]{:S(2)}) collective-permute-start(f32[2,3,3,3,48]{4,0,3,2,1:T(2,128)S(1)} %slice.3077), channel_id=1, source_target_pairs={{1,0},{0,1},{3,2},{2,3},{5,4},{4,5},{7,6},{6,7},{9,8},{8,9},{11,10... | collective-permute-start | bytes 31112 | tf_op jit(solution)/shard_map/ppermute | solution.py:14
  13.3 50.4 %collective-permute-start.6 = (f32[32,2,3,1,1152]{4,0,3,2,1:T(8,128)}, f32[32,2,3,1,1152]{4,0,3,2,1:T(8,128)}, u32[]{:S(2)}, u32[]{:S(2)}) collective-permute-start(f32[32,2,3,1,1152]{4,0,3,2,1:T(8,128)} %get-tuple-element.502), channel_id=1, source_target_pairs={{0,2},{2,0},{1,3},{3,1},{4,6},{6,4},{5,7},{7,5},{8,10},{10,8},{9,1... | collective-permute-start | bytes 2654216 | tf_op jit(solution)/shard_map/ppermute | solution.py:24
  16.0 49.7 %collective-permute-start.4 = (f32[32,2,3,1,1152]{4,0,3,2,1:T(8,128)}, f32[32,2,3,1,1152]{4,0,3,2,1:T(8,128)}, u32[]{:S(2)}, u32[]{:S(2)}) collective-permute-start(f32[32,2,3,1,1152]{4,0,3,2,1:T(8,128)} %get-tuple-element.503), channel_id=1, source_target_pairs={{2,0},{0,2},{3,1},{1,3},{6,4},{4,6},{7,5},{5,7},{10,8},{8,10},{11,... | collective-permute-start | bytes 2654216 | tf_op jit(solution)/shard_map/ppermute | solution.py:26
  18.8 1.4 copy-start.9
  18.8 1.4 copy-start.11
  18.8 1.4 copy-start.13
  18.9 1.4 copy-start.15
  24.1 33.0 %collective-permute-start.5 = (f32[2,3,3,1,1152]{4,0,3,2,1:T(2,128)}, f32[2,3,3,1,1152]{4,0,3,2,1:T(2,128)S(1)}, u32[]{:S(2)}, u32[]{:S(2)}) collective-permute-start(f32[2,3,3,1,1152]{4,0,3,2,1:T(2,128)} %slice.3143), channel_id=1, source_target_pairs={{2,0},{0,2},{3,1},{1,3},{6,4},{4,6},{7,5},{5,7},{10,8},{8,10},{11,... | collective-permute-start | bytes 248840 | tf_op jit(solution)/shard_map/ppermute | solution.py:14
  28.0 39.1 %collective-permute-start.1 = (f32[32,2,3,3,48]{4,0,3,2,1:T(8,128)}, f32[32,2,3,3,48]{4,0,3,2,1:T(8,128)S(1)}, u32[]{:S(2)}, u32[]{:S(2)}) collective-permute-start(f32[32,2,3,3,48]{4,0,3,2,1:T(8,128)} %get-tuple-element.509), channel_id=1, source_target_pairs={{1,0},{0,1},{3,2},{2,3},{5,4},{4,5},{7,6},{6,7},{9,8},{8,9},{11,10... | collective-permute-start | bytes 331784 | tf_op jit(solution)/shard_map/ppermute | solution.py:26
  62.7 2.3 copy-start.5
  71.7 1.7 copy-start.22
  76.5 22.6 %collective-permute-start.10 = (f32[32,2,3,1,1152]{4,0,3,2,1:T(8,128)S(1)}, f32[32,2,3,1,1152]{4,0,3,2,1:T(8,128)S(1)}, u32[]{:S(2)}, u32[]{:S(2)}) collective-permute-start(f32[32,2,3,1,1152]{4,0,3,2,1:T(8,128)S(1)} %get-tuple-element.493), channel_id=1, source_target_pairs={{0,2},{2,0},{1,3},{3,1},{4,6},{6,4},{5,7},{7,5},{8,10},{10,8},{9,1... | collective-permute-start | bytes 2654216 | tf_op jit(solution)/shard_map/ppermute | solution.py:24
  78.3 38.5 %collective-permute-start.9 = (f32[32,2,3,1,1152]{4,0,3,2,1:T(8,128)S(1)}, f32[32,2,3,1,1152]{4,0,3,2,1:T(8,128)S(1)}, u32[]{:S(2)}, u32[]{:S(2)}) collective-permute-start(f32[32,2,3,1,1152]{4,0,3,2,1:T(8,128)S(1)} %get-tuple-element.494), channel_id=1, source_target_pairs={{2,0},{0,2},{3,1},{1,3},{6,4},{4,6},{7,5},{5,7},{10,8},{8,10},{11,... | collective-permute-start | bytes 2654216 | tf_op jit(solution)/shard_map/ppermute | solution.py:26
  78.6 3.7 collective-permute-start.7
  78.6 3.7 collective-permute-start.8
  132.0 22.6 %collective-permute-start.13 = (f32[32,2,3,1,1152]{4,0,3,2,1:T(8,128)S(1)}, f32[32,2,3,1,1152]{4,0,3,2,1:T(8,128)S(1)}, u32[]{:S(2)}, u32[]{:S(2)}) collective-permute-start(f32[32,2,3,1,1152]{4,0,3,2,1:T(8,128)S(1)} %get-tuple-element.480), channel_id=1, source_target_pairs={{2,0},{0,2},{3,1},{1,3},{6,4},{4,6},{7,5},{5,7},{10,8},{8,10},{11,... | collective-permute-start | bytes 2654216 | tf_op jit(solution)/shard_map/ppermute | solution.py:26
  133.5 38.0 %collective-permute-start.14 = (f32[32,2,3,1,1152]{4,0,3,2,1:T(8,128)S(1)}, f32[32,2,3,1,1152]{4,0,3,2,1:T(8,128)S(1)}, u32[]{:S(2)}, u32[]{:S(2)}) collective-permute-start(f32[32,2,3,1,1152]{4,0,3,2,1:T(8,128)S(1)} %get-tuple-element.479), channel_id=1, source_target_pairs={{0,2},{2,0},{1,3},{3,1},{4,6},{6,4},{5,7},{7,5},{8,10},{10,8},{9,1... | collective-permute-start | bytes 2654216 | tf_op jit(solution)/shard_map/ppermute | solution.py:24
  134.0 2.7 collective-permute-start.11
  134.1 2.8 collective-permute-start.12
  186.7 22.6 %collective-permute-start.17 = (f32[32,2,3,1,1152]{4,0,3,2,1:T(8,128)S(1)}, f32[32,2,3,1,1152]{4,0,3,2,1:T(8,128)S(1)}, u32[]{:S(2)}, u32[]{:S(2)}) collective-permute-start(f32[32,2,3,1,1152]{4,0,3,2,1:T(8,128)S(1)} %get-tuple-element.466), channel_id=1, source_target_pairs={{2,0},{0,2},{3,1},{1,3},{6,4},{4,6},{7,5},{5,7},{10,8},{8,10},{11,... | collective-permute-start | bytes 2654216 | tf_op jit(solution)/shard_map/ppermute | solution.py:26
  187.9 37.4 %collective-permute-start.18 = (f32[32,2,3,1,1152]{4,0,3,2,1:T(8,128)S(1)}, f32[32,2,3,1,1152]{4,0,3,2,1:T(8,128)S(1)}, u32[]{:S(2)}, u32[]{:S(2)}) collective-permute-start(f32[32,2,3,1,1152]{4,0,3,2,1:T(8,128)S(1)} %get-tuple-element.465), channel_id=1, source_target_pairs={{0,2},{2,0},{1,3},{3,1},{4,6},{6,4},{5,7},{7,5},{8,10},{10,8},{9,1... | collective-permute-start | bytes 2654216 | tf_op jit(solution)/shard_map/ppermute | solution.py:24
  188.8 2.8 collective-permute-start.15
  188.8 2.8 collective-permute-start.16
  191.6 17.7 %copy-start.25 = (f32[32,2,3,3,48]{4,0,3,2,1:T(8,128)}, f32[32,2,3,3,48]{4,0,3,2,1:T(8,128)S(1)}, u32[]{:S(2)}) copy-start(f32[32,2,3,3,48]{4,0,3,2,1:T(8,128)S(1)} %collective-permute-done.15) | copy-start | bytes 331780
  191.6 17.7 %copy-start.28 = (f32[32,2,3,3,48]{4,0,3,2,1:T(8,128)}, f32[32,2,3,3,48]{4,0,3,2,1:T(8,128)S(1)}, u32[]{:S(2)}) copy-start(f32[32,2,3,3,48]{4,0,3,2,1:T(8,128)S(1)} %collective-permute-done.16) | copy-start | bytes 331780
  241.2 22.6 %collective-permute-start.21 = (f32[32,2,3,1,1152]{4,0,3,2,1:T(8,128)S(1)}, f32[32,2,3,1,1152]{4,0,3,2,1:T(8,128)S(1)}, u32[]{:S(2)}, u32[]{:S(2)}) collective-permute-start(f32[32,2,3,1,1152]{4,0,3,2,1:T(8,128)S(1)} %get-tuple-element.452), channel_id=1, source_target_pairs={{2,0},{0,2},{3,1},{1,3},{6,4},{4,6},{7,5},{5,7},{10,8},{8,10},{11,... | collective-permute-start | bytes 2654216 | tf_op jit(solution)/shard_map/ppermute | solution.py:26
  242.1 36.8 %collective-permute-start.22 = (f32[32,2,3,1,1152]{4,0,3,2,1:T(8,128)S(1)}, f32[32,2,3,1,1152]{4,0,3,2,1:T(8,128)S(1)}, u32[]{:S(2)}, u32[]{:S(2)}) collective-permute-start(f32[32,2,3,1,1152]{4,0,3,2,1:T(8,128)S(1)} %get-tuple-element.451), channel_id=1, source_target_pairs={{0,2},{2,0},{1,3},{3,1},{4,6},{6,4},{5,7},{7,5},{8,10},{10,8},{9,1... | collective-permute-start | bytes 2654216 | tf_op jit(solution)/shard_map/ppermute | solution.py:24
  243.3 2.8 collective-permute-start.19
  243.3 2.8 collective-permute-start.20
  293.6 22.6 %collective-permute-start.25 = (f32[32,2,3,1,1152]{4,0,3,2,1:T(8,128)S(1)}, f32[32,2,3,1,1152]{4,0,3,2,1:T(8,128)S(1)}, u32[]{:S(2)}, u32[]{:S(2)}) collective-permute-start(f32[32,2,3,1,1152]{4,0,3,2,1:T(8,128)S(1)} %get-tuple-element.438), channel_id=1, source_target_pairs={{2,0},{0,2},{3,1},{1,3},{6,4},{4,6},{7,5},{5,7},{10,8},{8,10},{11,... | collective-permute-start | bytes 2654216 | tf_op jit(solution)/shard_map/ppermute | solution.py:26
  294.3 36.2 %collective-permute-start.26 = (f32[32,2,3,1,1152]{4,0,3,2,1:T(8,128)S(1)}, f32[32,2,3,1,1152]{4,0,3,2,1:T(8,128)S(1)}, u32[]{:S(2)}, u32[]{:S(2)}) collective-permute-start(f32[32,2,3,1,1152]{4,0,3,2,1:T(8,128)S(1)} %get-tuple-element.437), channel_id=1, source_target_pairs={{0,2},{2,0},{1,3},{3,1},{4,6},{6,4},{5,7},{7,5},{8,10},{10,8},{9,1... | collective-permute-start | bytes 2654216 | tf_op jit(solution)/shard_map/ppermute | solution.py:24
  295.7 2.8 collective-permute-start.23
  295.7 2.8 collective-permute-start.24
  345.8 22.6 %collective-permute-start.29 = (f32[32,2,3,1,1152]{4,0,3,2,1:T(8,128)S(1)}, f32[32,2,3,1,1152]{4,0,3,2,1:T(8,128)S(1)}, u32[]{:S(2)}, u32[]{:S(2)}) collective-permute-start(f32[32,2,3,1,1152]{4,0,3,2,1:T(8,128)S(1)} %get-tuple-element.424), channel_id=1, source_target_pairs={{2,0},{0,2},{3,1},{1,3},{6,4},{4,6},{7,5},{5,7},{10,8},{8,10},{11,... | collective-permute-start | bytes 2654216 | tf_op jit(solution)/shard_map/ppermute | solution.py:26
  346.2 35.7 %collective-permute-start.30 = (f32[32,2,3,1,1152]{4,0,3,2,1:T(8,128)S(1)}, f32[32,2,3,1,1152]{4,0,3,2,1:T(8,128)S(1)}, u32[]{:S(2)}, u32[]{:S(2)}) collective-permute-start(f32[32,2,3,1,1152]{4,0,3,2,1:T(8,128)S(1)} %get-tuple-element.423), channel_id=1, source_target_pairs={{0,2},{2,0},{1,3},{3,1},{4,6},{6,4},{5,7},{7,5},{8,10},{10,8},{9,1... | collective-permute-start | bytes 2654216 | tf_op jit(solution)/shard_map/ppermute | solution.py:24
  347.8 2.8 collective-permute-start.27
  347.8 2.8 collective-permute-start.28
  350.6 17.7 %copy-start.26 = (f32[32,2,3,3,48]{4,0,3,2,1:T(8,128)}, f32[32,2,3,3,48]{4,0,3,2,1:T(8,128)S(1)}, u32[]{:S(2)}) copy-start(f32[32,2,3,3,48]{4,0,3,2,1:T(8,128)S(1)} %collective-permute-done.27) | copy-start | bytes 331780
  350.7 17.7 %copy-start.29 = (f32[32,2,3,3,48]{4,0,3,2,1:T(8,128)}, f32[32,2,3,3,48]{4,0,3,2,1:T(8,128)S(1)}, u32[]{:S(2)}) copy-start(f32[32,2,3,3,48]{4,0,3,2,1:T(8,128)S(1)} %collective-permute-done.28) | copy-start | bytes 331780
  397.9 22.6 %collective-permute-start.33 = (f32[32,2,3,1,1152]{4,0,3,2,1:T(8,128)S(1)}, f32[32,2,3,1,1152]{4,0,3,2,1:T(8,128)S(1)}, u32[]{:S(2)}, u32[]{:S(2)}) collective-permute-start(f32[32,2,3,1,1152]{4,0,3,2,1:T(8,128)S(1)} %get-tuple-element.410), channel_id=1, source_target_pairs={{2,0},{0,2},{3,1},{1,3},{6,4},{4,6},{7,5},{5,7},{10,8},{8,10},{11,... | collective-permute-start | bytes 2654216 | tf_op jit(solution)/shard_map/ppermute | solution.py:26
  398.3 34.9 %collective-permute-start.34 = (f32[32,2,3,1,1152]{4,0,3,2,1:T(8,128)S(1)}, f32[32,2,3,1,1152]{4,0,3,2,1:T(8,128)S(1)}, u32[]{:S(2)}, u32[]{:S(2)}) collective-permute-start(f32[32,2,3,1,1152]{4,0,3,2,1:T(8,128)S(1)} %get-tuple-element.409), channel_id=1, source_target_pairs={{0,2},{2,0},{1,3},{3,1},{4,6},{6,4},{5,7},{7,5},{8,10},{10,8},{9,1... | collective-permute-start | bytes 2654216 | tf_op jit(solution)/shard_map/ppermute | solution.py:24
  400.0 2.8 collective-permute-start.31
  400.0 2.8 collective-permute-start.32
  402.8 17.7 %copy-start.27 = (f32[32,2,3,3,48]{4,0,3,2,1:T(8,128)}, f32[32,2,3,3,48]{4,0,3,2,1:T(8,128)S(1)}, u32[]{:S(2)}) copy-start(f32[32,2,3,3,48]{4,0,3,2,1:T(8,128)S(1)} %collective-permute-done.31) | copy-start | bytes 331780
  402.8 17.7 %copy-start.30 = (f32[32,2,3,3,48]{4,0,3,2,1:T(8,128)}, f32[32,2,3,3,48]{4,0,3,2,1:T(8,128)S(1)}, u32[]{:S(2)}) copy-start(f32[32,2,3,3,48]{4,0,3,2,1:T(8,128)S(1)} %collective-permute-done.32) | copy-start | bytes 331780
  447.6 45.1 %copy-start = (f32[32,2,3,3,1152]{4,0,3,2,1:T(8,128)}, f32[32,2,3,3,1152]{4,0,3,2,1:T(8,128)S(1)}, u32[]{:S(2)}) copy-start(f32[32,2,3,3,1152]{4,0,3,2,1:T(8,128)S(1)} %fusion.144) | copy-start | bytes 7962628
  448.8 22.6 %collective-permute-start.37 = (f32[32,2,3,1,1152]{4,0,3,2,1:T(8,128)S(1)}, f32[32,2,3,1,1152]{4,0,3,2,1:T(8,128)S(1)}, u32[]{:S(2)}, u32[]{:S(2)}) collective-permute-start(f32[32,2,3,1,1152]{4,0,3,2,1:T(8,128)S(1)} %get-tuple-element.396), channel_id=1, source_target_pairs={{2,0},{0,2},{3,1},{1,3},{6,4},{4,6},{7,5},{5,7},{10,8},{8,10},{11,... | collective-permute-start | bytes 2654216 | tf_op jit(solution)/shard_map/ppermute | solution.py:26
  449.2 34.0 %collective-permute-start.38 = (f32[32,2,3,1,1152]{4,0,3,2,1:T(8,128)S(1)}, f32[32,2,3,1,1152]{4,0,3,2,1:T(8,128)S(1)}, u32[]{:S(2)}, u32[]{:S(2)}) collective-permute-start(f32[32,2,3,1,1152]{4,0,3,2,1:T(8,128)S(1)} %get-tuple-element.395), channel_id=1, source_target_pairs={{0,2},{2,0},{1,3},{3,1},{4,6},{6,4},{5,7},{7,5},{8,10},{10,8},{9,1... | collective-permute-start | bytes 2654216 | tf_op jit(solution)/shard_map/ppermute | solution.py:24
  450.9 4.3 collective-permute-start.35
  450.9 4.3 collective-permute-start.36
  498.2 56.0 %collective-permute-start = (f32[32,2,3,3,1152]{4,0,3,2,1:T(8,128)S(1)}, f32[32,2,3,3,1152]{4,0,3,2,1:T(8,128)}, u32[]{:S(2)}, u32[]{:S(2)}) collective-permute-start(f32[32,2,3,3,1152]{4,0,3,2,1:T(8,128)S(1)} %copy.138), channel_id=1, source_target_pairs={{12,0},{0,4},{4,8},{8,12},{13,1},{1,5},{5,9},{9,13},{14,2},{2,6},{... | collective-permute-start | bytes 7962632 | tf_op jit(solution)/shard_map/while/body/eval_jaxpr/ppermute | solution.py:14
  498.2 2.8 copy-start.3
  505.3 2.8 copy-start.1
  556.0 56.0 %collective-permute-start = (f32[32,2,3,3,1152]{4,0,3,2,1:T(8,128)S(1)}, f32[32,2,3,3,1152]{4,0,3,2,1:T(8,128)}, u32[]{:S(2)}, u32[]{:S(2)}) collective-permute-start(f32[32,2,3,3,1152]{4,0,3,2,1:T(8,128)S(1)} %copy.138), channel_id=1, source_target_pairs={{12,0},{0,4},{4,8},{8,12},{13,1},{1,5},{5,9},{9,13},{14,2},{2,6},{... | collective-permute-start | bytes 7962632 | tf_op jit(solution)/shard_map/while/body/eval_jaxpr/ppermute | solution.py:14
  556.0 2.8 copy-start.3
  563.3 2.8 copy-start.1
  613.7 52.6 %collective-permute-start = (f32[32,2,3,3,1152]{4,0,3,2,1:T(8,128)S(1)}, f32[32,2,3,3,1152]{4,0,3,2,1:T(8,128)}, u32[]{:S(2)}, u32[]{:S(2)}) collective-permute-start(f32[32,2,3,3,1152]{4,0,3,2,1:T(8,128)S(1)} %copy.138), channel_id=1, source_target_pairs={{12,0},{0,4},{4,8},{8,12},{13,1},{1,5},{5,9},{9,13},{14,2},{2,6},{... | collective-permute-start | bytes 7962632 | tf_op jit(solution)/shard_map/while/body/eval_jaxpr/ppermute | solution.py:14
  613.7 2.8 copy-start.3
  621.0 2.8 copy-start.1
  666.5 3.2 copy-start.4
  669.7 2.8 copy-start.2
  (15 other events, 13.7 us)
Sparse Core Ops, SparseCore 0:
  690.3 28.2 all-reduce.2
where the time goes:
time: 739 us; the launch traced here: 729 us
  waiting for transfers between devices  432 us (58%)
  other arithmetic  138 us (19%)
  matrix products  62.1 us (8%)
  local copies, waits for them, and re-layouts  51.6 us (7%)
  starting transfers between devices  26.5 us (4%)
  between operations  16.8 us (2%)
    ppermute x5, waiting for transfers between devices, from_behind(): return lax.ppermute(block, axis, route)  150 us
    ppermute x18, waiting for transfers between devices, with_halo(): lax.ppermute(head, axis, [((i + 1) % count, i) for i in range(count)])  140 us
    ppermute x18, waiting for transfers between devices, with_halo(): lax.ppermute(tail, axis, [(i, (i + 1) % count) for i in range(count)])  117 us
    dot_general x32, matrix products, inner_product(): lax.dot_general(left_matrix, right_matrix, (((1,), (1,)), ((), ())), prec...  62.1 us
    add x54, other arithmetic, apply_link(): out_real + (mat_real[None] * src_real - mat_imag[None] * src_imag)  56.9 us
    squeeze x9, other arithmetic, apply_link(): vec_real = source[:, 0]  25 us
    psum x1, waiting for transfers between devices, body(): gram_rows, image_rows = lax.psum((gram_rows, image_rows), ('space', 'rep'))  24.8 us
    sub x7, other arithmetic, chebyshev(): following = 2.0 * filter_map(current) - previous  24.2 us
  transfers between devices with their start and end apart: 42, of which 21 were waited for; matrix products, arithmetic and copies ran while one was open for 12% of the time, Pallas kernels for 0%

commit v1 on v0

v1 whole, which is shorter than its diff:
```python
import functools

import jax
import jax.numpy as jnp
from jax import lax
from jax.experimental import pallas as pl
from jax.experimental.pallas import tpu as pltpu
from jax.sharding import PartitionSpec as P

LX = 48
LY = 48
DEG = 8
LANES = 128


def shift_y(block, forward):
    width = block.shape[-1]
    position = lax.broadcasted_iota(jnp.int32, block.shape, 1) % LY
    if forward:
        return jnp.where(
            position == LY - 1,
            pltpu.roll(block, LY - 1, 1),
            pltpu.roll(block, width - 1, 1),
        )
    return jnp.where(
        position == 0, pltpu.roll(block, width - LY + 1, 1), pltpu.roll(block, 1, 1)
    )


def shift_x(block, forward):
    width = block.shape[-1]
    return pltpu.roll(block, width - LY if forward else LY, 1)


def prepare_links(links_ref, made_ref, planes):
    def one(z, carry):
        for mu in range(3):
            real = links_ref[z, mu * 2]
            imag = links_ref[z, mu * 2 + 1]
            sources = [(mu, real, imag)]
            if mu == 0:
                sources.append((3, shift_x(real, False), shift_x(imag, False)))
            if mu == 1:
                sources.append((4, shift_y(real, False), shift_y(imag, False)))
            for slot, a, b in sources:
                made_ref[z, slot * 3] = a
                made_ref[z, slot * 3 + 1] = b - a
                made_ref[z, slot * 3 + 2] = a + b
        return carry

    lax.fori_loop(0, planes, one, 0)


def hop_pass(source_ref, made_ref, moved_ref, planes, width, emit):
    def plane(z, carry):
        def move(comp, inner):
            field = source_ref[comp * planes + z]
            moved_ref[comp] = shift_x(field, True)
            moved_ref[6 + comp] = shift_y(field, True)
            moved_ref[12 + comp] = shift_x(field, False)
            moved_ref[18 + comp] = shift_y(field, False)
            return inner

        lax.fori_loop(0, 6, move, 0)
        ahead = lax.rem(z + 1, planes)
        behind = lax.rem(z + planes - 1, planes)

        def chunk(j, inner):
            lanes = pl.ds(pl.multiple_of(j * LANES, LANES), LANES)
            one = [None] * 3
            two = [None] * 3
            three = [None] * 3

            def add(total, term):
                return term if total is None else total + term

            def sub(total, term):
                return -term if total is None else total - term

            terms = (
                (0, z, lambda c: moved_ref[c, :, lanes], False),
                (1, z, lambda c: moved_ref[6 + c, :, lanes], False),
                (2, z, lambda c: source_ref[c * planes + ahead, :, lanes], False),
                (3, z, lambda c: moved_ref[12 + c, :, lanes], True),
                (4, z, lambda c: moved_ref[18 + c, :, lanes], True),
                (2, behind, lambda c: source_ref[c * planes + behind, :, lanes], True),
            )
            for slot, link_plane, load, dagger in terms:
                for col in range(3):
                    x = load(col)
                    y = load(3 + col)
                    both = x + y
                    for row in range(3):
                        entry = col * 3 + row if dagger else row * 3 + col
                        at = slice(entry, entry + 1)
                        a = made_ref[link_plane, slot * 3, at, lanes]
                        m = made_ref[link_plane, slot * 3 + 1, at, lanes]
                        p = made_ref[link_plane, slot * 3 + 2, at, lanes]
                        one[row] = add(one[row], a * both)
                        if dagger:
                            two[row] = sub(two[row], p * x)
                            three[row] = sub(three[row], m * y)
                        else:
                            two[row] = add(two[row], m * x)
                            three[row] = add(three[row], p * y)
            for row in range(3):
                emit(row * planes + z, lanes, one[row] - three[row])
                emit((3 + row) * planes + z, lanes, one[row] + two[row])
            return inner

        lax.fori_loop(0, width // LANES, chunk, 0)
        return carry

    lax.fori_loop(0, planes, plane, 0)


def filter_kernel(planes, width, start_ref, links_ref, out_ref, made_ref, fields_ref, moved_ref):
    prepare_links(links_ref, made_ref, planes)

    def fill(i, carry):
        fields_ref[0, i] = start_ref[i]
        fields_ref[1, i] = jnp.zeros_like(start_ref[i])
        return carry

    lax.fori_loop(0, 6 * planes, fill, 0)

    def step(k, carry):
        now = lax.rem(k, 2)
        later = 1 - now
        scale = jnp.where(k == 0, -1.0 / 11.0, -2.0 / 11.0).astype(jnp.float32)
        current = fields_ref.at[now]
        target = fields_ref.at[later]

        def emit(i, lanes, hop):
            target[i, :, lanes] = scale * (current[i, :, lanes] + 2.0 * hop) - target[i, :, lanes]

        hop_pass(current, made_ref, moved_ref, planes, width, emit)
        return carry

    lax.fori_loop(0, DEG, step, 0)

    def leave(i, carry):
        out_ref[i] = fields_ref[DEG % 2, i]
        return carry

    lax.fori_loop(0, 6 * planes, leave, 0)


def image_kernel(planes, width, field_ref, links_ref, out_ref, made_ref, moved_ref):
    prepare_links(links_ref, made_ref, planes)

    def emit(i, lanes, hop):
        out_ref[i, :, lanes] = 6.0 * field_ref[i, :, lanes] - hop

    hop_pass(field_ref, made_ref, moved_ref, planes, width, emit)


def run_kernel(kernel, field, links, planes, with_fields):
    _, count, width = field.shape
    scratch = [pltpu.VMEM((planes, 15, 9, width), jnp.float32)]
    if with_fields:
        scratch.append(pltpu.VMEM((2,) + field.shape, jnp.float32))
    scratch.append(pltpu.VMEM((24, count, width), jnp.float32))
    return pl.pallas_call(
        functools.partial(kernel, planes, width),
        out_shape=jax.ShapeDtypeStruct(field.shape, jnp.float32),
        in_specs=[pl.BlockSpec(memory_space=pltpu.VMEM)] * 2,
        out_specs=pl.BlockSpec(memory_space=pltpu.VMEM),
        scratch_shapes=scratch,
        compiler_params=pltpu.CompilerParams(vmem_limit_bytes=60 * 1024 * 1024),
    )(field, links)


def inner_product(left_matrix, right_matrix):
    return lax.dot_general(
        left_matrix,
        right_matrix,
        (((1,), (1,)), ((), ())),
        precision=lax.Precision.HIGH,
        preferred_element_type=jnp.float32,
    )


def body(colour_vectors, gauge_links):
    local_count, _, _, local_z, local_x = colour_vectors.shape
    space = lax.axis_size("space")
    rep = lax.axis_size("rep")
    group = space * rep
    count = local_count // group
    planes = local_z * space
    width = local_x * rep
    both = ("space", "rep")

    links = lax.all_gather(gauge_links, "space", axis=4, tiled=True)
    links = lax.all_gather(links, "rep", axis=5, tiled=True)
    links = links.reshape(6, 9, planes, width).transpose(2, 0, 1, 3)

    start = lax.all_to_all(
        colour_vectors.reshape(space, rep, count, 6, local_z, local_x).reshape(
            group, count, 6, local_z, local_x
        ),
        both,
        0,
        0,
    )
    start = start.reshape(space, rep, count, 6, local_z, local_x)
    start = start.transpose(3, 0, 4, 2, 1, 5).reshape(6 * planes, count, width)

    def home(field):
        field = field.reshape(6, space, local_z, count, rep, local_x)
        field = field.transpose(1, 4, 3, 0, 2, 5).reshape(group, count, 6, local_z, local_x)
        field = lax.all_to_all(field, both, 0, 0)
        return field.reshape(local_count, 2, 3, local_z, local_x)

    whole_filtered = run_kernel(filter_kernel, start, links, planes, True)
    filtered = home(whole_filtered)
    whole_image = run_kernel(image_kernel, whole_filtered, links, planes, False)
    image = home(whole_image)

    site_count = float(width * planes)
    panel = filtered.reshape(local_count, 2, -1)
    panels = lax.all_gather(panel, "vec", axis=0, tiled=True)
    rows = jnp.concatenate([panel, image.reshape(local_count, 2, -1)], axis=0)

    real_part = inner_product(rows[:, 0], panels[:, 0]) + inner_product(rows[:, 1], panels[:, 1])
    imag_part = inner_product(rows[:, 0], panels[:, 1]) - inner_product(rows[:, 1], panels[:, 0])
    result = lax.psum(jnp.stack([real_part, imag_part]), both) / site_count
    return (filtered, result[:, :local_count], result[:, local_count:])


def solution(mesh):
    return jax.shard_map(
        body,
        mesh=mesh,
        in_specs=(
            P(("cuts", "vec"), None, None, "space", "rep"),
            P(None, None, None, None, ("cuts", "space"), "rep"),
        ),
        out_specs=(
            P(("cuts", "vec"), None, None, "space", "rep"),
            P(None, ("cuts", "vec"), None),
            P(None, ("cuts", "vec"), None),
        ),
        check_vma=False,
    )
```

time: 739 us -> 505 us (0.68); the launches traced: 729 us -> 504 us
  waiting for transfers between devices: 432 us -> 161 us
  Pallas kernels: 0 us -> 144 us
  other arithmetic: 138 us -> 1.49 us
  blocking collectives: 0 us -> 102 us
  matrix products: 62.1 us -> 11.5 us
  starting transfers between devices: 26.5 us -> 0.16 us
  local copies, waits for them, and re-layouts: 51.6 us -> 69.6 us
    ppermute x41 -> x0, waiting for transfers between devices: 407 us -> none  [the longest x5 150 us: from_behind(): return lax.ppermute(block, axis, route)]
    pallas_call x0 -> x2, Pallas kernels: none -> 144 us  [run_kernel(): pl.pallas_call(functools.partial(kernel, planes, width), out_shape=jax.Sh...]
    all_gather x0 -> x3, waiting for transfers between devices: none -> 134 us  [the longest x1 103 us: body(): panels = lax.all_gather(panel, 'vec', axis=0, tiled=True)]
    all_to_all x0 -> x3, blocking collectives: none -> 102 us  [the longest x2 68.2 us: home(): field = lax.all_to_all(field, both, 0, 0)]
    add x54 -> x0, other arithmetic: 56.9 us -> none  [apply_link(): out_real + (mat_real[None] * src_real - mat_imag[None] * src_imag)]
    dot_general x32 -> x4, matrix products: 62.1 us -> 11.5 us  [inner_product(): lax.dot_general(left_matrix, right_matrix, (((1,), (1,)), ((), ())), prec...]
    sub x8 -> x0, other arithmetic: 27.8 us -> none  [the longest x7 24.2 us: chebyshev(): following = 2.0 * filter_map(current) - previous]
    ppermute x41 -> x0, starting transfers between devices: 26.5 us -> none  [the longest x18 18.1 us: with_halo(): lax.ppermute(tail, axis, [(i, (i + 1) % count) for i in range(count)])]
  transfers between devices with their start and end apart: 42 -> 4, of which waited for: 21 -> 3; matrix products, arithmetic and copies ran while one was open for 12% -> 7% of each run, Pallas kernels for 0% -> 4%
where the time goes in v1:
time: 505 us; the launch traced here: 504 us
  waiting for transfers between devices  161 us (32%)
  Pallas kernels  144 us (29%)
  blocking collectives  102 us (20%)
  local copies, waits for them, and re-layouts  69.6 us (14%)
  between operations  13.8 us (3%)
  matrix products  11.5 us (2%)
    pallas_call x2, Pallas kernels, run_kernel(): pl.pallas_call(functools.partial(kernel, planes, width), out_shape=jax.Sh...  144 us
    all_gather x1, waiting for transfers between devices, body(): panels = lax.all_gather(panel, 'vec', axis=0, tiled=True)  103 us
    all_to_all x2, blocking collectives, home(): field = lax.all_to_all(field, both, 0, 0)  68.2 us
    all_to_all x1, blocking collectives, body(): lax.all_to_all(colour_vectors.reshape(space, rep, count, 6, local_z, loca...  34.1 us
    all_gather x1, waiting for transfers between devices, body(): links = lax.all_gather(gauge_links, 'space', axis=4, tiled=True)  30.6 us
    psum x1, waiting for transfers between devices, body(): result = lax.psum(jnp.stack([real_part, imag_part]), both) / site_count  26 us
    slice x1, local copies, waits for them, and re-layouts, body(): panels[:, 0]  12.5 us
    dot_general x4, matrix products, inner_product(): lax.dot_general(left_matrix, right_matrix, (((1,), (1,)), ((), ())), prec...  11.5 us
  transfers between devices with their start and end apart: 4, of which 3 were waited for; matrix products, arithmetic and copies ran while one was open for 7% of the time, Pallas kernels for 4%

profile of v1, /device:TPU:0, one launch (start us, length us, event | category | flops | bytes accessed | tf_op | source)
XLA Modules:
  0.0 504.0 jit_solution(11793512148128142115)
XLA Ops:
  7.2 0.0 all-gather.4.cloned.1.call-start
  7.2 0.7 all-gather.4.cloned.1.call-update
  7.9 0.0 all-gather.6.cloned.1.call-start
  7.9 30.6 %all-gather.4.cloned.1.call-done = f32[3,2,3,3,6,1152]{5,1,4,3,2,0:T(2,128)} async-done(((f32[3,2,3,3,3,1152]{5,1,4,3,2,0:T(2,128)}), f32[3,2,3,3,6,1152]{5,1,4,3,2,0:T(2,128)}) %all-gather.4.cloned.1.call-update) | async-done | bytes 1493008 | tf_op jit(solution)/shard_map/all_gather | solution.py:194
  38.6 0.0 all-gather.6.cloned.1.call-update
  38.6 0.0 all-gather.8.cloned.1.call-start
  38.6 2.0 copy.17
  40.7 0.2 copy.18
  40.9 34.1 %all_to_all.15 = f32[4,8,6,3,1152]{4,1,3,2,0:T(8,128)S(1)} all-to-all(f32[4,8,6,3,1152]{4,1,3,2,0:T(8,128)S(1)} %copy.18), channel_id=1, replica_groups=mesh['cuts'=2,'vec'=4,'space'=2,'rep'=2] {'space','rep'}, dimensions={0} | all-to-all | bytes 5308416 | tf_op jit(solution)/shard_map/all_to_all | solution.py:198
  75.0 1.7 copy.19
  76.7 0.0 all-gather.6.cloned.1.call-done
  76.7 4.7 copy.28
  81.4 6.5 %reshape.38 = f32[6,9,6,2304]{3,1,0,2:T(8,128)} reshape(f32[3,2,3,3,6,2304]{5,3,2,1,0,4:T(4,128)} %copy.28) | data formatting | bytes 5971968 | tf_op jit(solution)/shard_map/reshape | solution.py:196
  87.9 122.8 %shard_map.49.field_ref = f32[36,8,2304]{2,1,0:T(8,128)} custom-call(f32[36,8,2304]{2,1,0:T(8,128)} %bitcast.65, f32[6,6,9,2304]{3,2,1,0:T(8,128)} %bitcast.57), custom_call_target="tpu_custom_call" | custom-call | tf_op jit(solution)/shard_map/pallas_call | solution.py:164
  210.7 1.9 copy.22
  212.6 34.1 %all_to_all.16 = f32[4,8,6,3,1152]{4,1,3,2,0:T(8,128)S(1)} all-to-all(f32[4,8,6,3,1152]{4,1,3,2,0:T(8,128)S(1)} %bitcast.64), channel_id=1, replica_groups=mesh['cuts'=2,'vec'=4,'space'=2,'rep'=2] {'space','rep'}, dimensions={0} | all-to-all | bytes 5308416 | tf_op jit(solution)/shard_map/all_to_all | solution.py:212
  246.7 2.7 copy.24
  249.4 5.9 %reshape_reshape.10 = f32[32,2,10368]{2,1,0:T(2,128)} reshape(f32[4,8,6,3,1152]{4,3,2,1,0:T(4,128)} %copy.24) | data formatting | bytes 5308416 | tf_op jit(solution)/shard_map/reshape;reshape | solution.py:221
  255.2 0.0 all-gather.8.cloned.1.call-update
  255.2 0.0 all-reduce.2.cloned.1.call-start
  255.3 21.7 %shard_map.50 = f32[36,8,2304]{2,1,0:T(8,128)} custom-call(f32[36,8,2304]{2,1,0:T(8,128)} %shard_map.49.field_ref, f32[6,6,9,2304]{3,2,1,0:T(8,128)} %bitcast.58), custom_call_target="tpu_custom_call" | custom-call | tf_op jit(solution)/shard_map/pallas_call | solution.py:164
  276.9 1.9 copy.25
  278.9 34.1 %all_to_all.17 = f32[4,8,6,3,1152]{4,1,3,2,0:T(8,128)S(1)} all-to-all(f32[4,8,6,3,1152]{4,1,3,2,0:T(8,128)S(1)} %bitcast.61), channel_id=1, replica_groups=mesh['cuts'=2,'vec'=4,'space'=2,'rep'=2] {'space','rep'}, dimensions={0} | all-to-all | bytes 5308416 | tf_op jit(solution)/shard_map/all_to_all | solution.py:212
  313.0 2.8 copy.26
  315.8 5.9 %reshape_reshape.11 = f32[32,2,10368]{2,1,0:T(2,128)} reshape(f32[4,8,6,3,1152]{4,3,2,1,0:T(4,128)} %copy.26) | data formatting | bytes 5308416 | tf_op jit(solution)/shard_map/reshape;reshape | solution.py:223
  321.7 0.0 copy-start.2
  321.7 3.7 constant_dynamic-update-slice_fusion.1
  325.3 0.0 copy-done.2
  325.4 1.7 constant_dynamic-update-slice_fusion
  327.0 11.1 %fusion.41 = (f32[64,1,10368]{2,1,0:T(1,128)}, f32[64,1,10368]{2,1,0:T(1,128)}) fusion(f32[64,2,10368]{2,1,0:T(2,128)} %constant_dynamic-update-slice_fusion), kind=kLoop, calls=%fused_computation.29 | loop fusion | bytes 10616832 | tf_op jit(solution)/shard_map/slice | solution.py:225
  338.1 103.3 %all-gather.8.cloned.1.call-done = f32[128,2,10368]{2,1,0:T(2,128)} async-done(((f32[32,2,10368]{2,1,0:T(2,128)}), f32[128,2,10368]{2,1,0:T(2,128)}) %all-gather.8.cloned.1.call-update) | async-done | bytes 10616848 | tf_op jit(solution)/shard_map/all_gather | solution.py:222
  441.4 0.0 copy-start
  441.4 12.5 %fusion.40 = (f32[128,1,10368]{2,1,0:T(1,128)S(1)}, f32[128,1,10368]{2,1,0:T(1,128)S(1)}) fusion(f32[128,2,10368]{2,1,0:T(2,128)} %all-gather.8.cloned.1.call-done), kind=kLoop, calls=%fused_computation.28 | loop fusion | bytes 21233664 | tf_op jit(solution)/shard_map/slice | solution.py:225
  453.9 0.0 copy-done
  453.9 0.0 copy-start.1
  453.9 2.9 fusion.2
  456.8 0.0 copy-done.1
  456.8 2.9 fusion
  459.7 2.9 fusion.25
  462.6 2.9 fusion.35
  465.5 0.6 pad_maximum_fusion
  466.1 0.0 all-reduce.2.cloned.1.call-update
  466.1 0.3 copy.23
  466.4 3.6 copy.27
  470.0 26.0 %all-reduce.2.cloned.1.call-done = f32[2,64,128]{2,1,0:T(8,128)} async-done(((f32[2,64,128]{2,1,0:T(8,128)}), f32[2,64,128]{2,1,0:T(8,128)}) %all-reduce.2.cloned.1.call-update) | async-done | bytes 65552 | tf_op jit(solution)/shard_map/psum | solution.py:227
  496.0 0.8 broadcast_multiply_fusion
  496.9 0.6 fusion.42
Async XLA Ops:
  7.2 31.4 %all-gather.4.cloned.1.call-start = ((), (), s32[]{:S(2)}) async-start(), calls=%async_computation.3 | async-start | bytes 2239488 | tf_op jit(solution)/shard_map/all_gather | solution.py:194
  7.9 68.8 %all-gather.6.cloned.1.call-start = ((), (), s32[]{:S(2)}) async-start(), calls=%async_computation.4 | async-start | bytes 4478976 | tf_op jit(solution)/shard_map/all_gather | solution.py:195
  38.6 402.9 %all-gather.8.cloned.1.call-start = ((), (), s32[]{:S(2)}) async-start(), calls=%async_computation.5 | async-start | bytes 13271040 | tf_op jit(solution)/shard_map/all_gather | solution.py:222
  255.2 240.8 %all-reduce.2.cloned.1.call-start = ((), (), s32[]{:S(2)}) async-start(), calls=%async_computation.6 | async-start | bytes 131072 | tf_op jit(solution)/shard_map/psum | solution.py:227
  321.7 3.7 copy-start.2
  441.4 12.5 %copy-start = (f32[64,1,10368]{2,1,0:T(1,128)S(1)}, f32[64,1,10368]{2,1,0:T(1,128)}, u32[]{:S(2)}) copy-start(f32[64,1,10368]{2,1,0:T(1,128)} %get-tuple-element.11) | copy-start | bytes 7962628
  453.9 2.9 copy-start.1
Sparse Core Ops, SparseCore 0:
  9.5 28.9 all-gather.3
  40.1 11.7 all-gather.5
  255.4 186.0 all-gather.7
  466.3 29.7 all-reduce.1
